TPU v7x, 32 devices: a whole 2x2x4 slice. The times are simulated.
32 devices in a mesh: expert: 8 (over y, x, core), tensor: 4 (over z).
Axes of the slice: x: 2, y: 2, z: 4, core: 2. Of those that a mesh axis runs over, the one named last changes fastest.
Arguments:
- grad_out: bfloat16 [1024, 4096], P('expert', 'tensor'), may hold values from -6 to 6
- expert_ids: int32 [1024, 4], P('expert'), may hold values from 0 to 7, all different within a row
- gate_probs: float32 [1024, 4], P('expert'), may hold values from 0.05 to 0.6
- live: int32 [1024], P('expert'), may hold values 0 or 1
- w_gate: bfloat16 [8, 5376, 4096], P('expert', 'tensor'), may hold values from -0.09375 to 0.09375
- w_up: bfloat16 [8, 5376, 4096], P('expert', 'tensor'), may hold values from -0.09375 to 0.09375
- w_down: bfloat16 [8, 5376, 4096], P('expert', 'tensor'), may hold values from -0.078125 to 0.078125
- saved: bfloat16 [8, 2, 5376, 512], P('expert', None, 'tensor'), may hold values from -8 to 8
Outputs:
- grad_in: bfloat16 [1024, 4096], P('expert', 'tensor')
Inputs may be any that keep to these rules, and one draw needn't show every extreme that they name: `expert_ids`: the 4 ids of a token are different.
All inputs are finite; a program needn't handle non-finite values. No bound on the sum of `live` on one device may be relied on, other than what follows from the above.
Results may differ from a plain program's by a relative error of at most 0.012.
Values may be sent and summed in bfloat16 or wider, within the bound.
A program may use at most 128 MiB of HBM per device.

v0:
```python
import jax
import jax.numpy as jnp
from jax import lax
from jax.sharding import PartitionSpec as P


def shards(grad_out, expert_ids, gate_probs, live, w_gate, w_up, w_down, saved):
    tokens_here = grad_out.shape[0]
    top_count = expert_ids.shape[1]
    groups = lax.axis_size("expert")
    assignments = tokens_here * top_count
    capacity = assignments // groups
    flat_ids = expert_ids.reshape(-1)
    alive = jnp.repeat(live, top_count)
    onehot = (flat_ids[:, None] == jnp.arange(groups, dtype=jnp.int32)[None, :]).astype(
        jnp.int32
    ) * alive[:, None]
    position = jnp.sum((jnp.cumsum(onehot, axis=0) - onehot) * onehot, axis=1)
    kept = (jnp.sum(onehot, axis=1) > 0) & (position < capacity)
    target = flat_ids * capacity + position
    select = (
        (target[:, None] == jnp.arange(assignments, dtype=jnp.int32)[None, :]) & kept[:, None]
    ).astype(jnp.bfloat16)
    factors = gate_probs.reshape(-1)[:, None]
    down_rows = w_down[0]
    contract_inner = (((1,), (1,)), ((), ()))
    contract_outer = (((0,), (0,)), ((), ()))
    repeated = jnp.repeat(grad_out, top_count, axis=0)
    scaled = (factors * repeated.astype(jnp.float32)).astype(jnp.bfloat16)
    outgoing = lax.dot_general(
        select, scaled, contract_outer, preferred_element_type=jnp.float32
    ).astype(jnp.bfloat16)
    arrived = lax.all_to_all(
        outgoing.reshape(groups, capacity, -1), "expert", split_axis=0, concat_axis=0, tiled=True
    )
    arrived = arrived.reshape(assignments, -1)
    grad_hidden = lax.dot_general(
        down_rows,
        lax.all_gather(arrived, "tensor", axis=1, tiled=True),
        contract_inner,
        preferred_element_type=jnp.float32,
    )
    pre_gate = saved[0, 0].astype(jnp.float32)
    pre_up = saved[0, 1].astype(jnp.float32)
    sigma = jax.nn.sigmoid(pre_gate)
    d_up = (grad_hidden * pre_gate * sigma).astype(jnp.bfloat16)
    d_gate = (grad_hidden * pre_up * sigma * (1.0 + pre_gate * (1.0 - sigma))).astype(jnp.bfloat16)
    gate_rows = w_gate[0]
    up_rows = w_up[0]
    collect = jnp.sum(
        select.reshape(tokens_here, top_count, assignments).astype(jnp.float32), axis=1
    )
    feature_share = gate_rows.shape[1] // lax.axis_size("tensor")
    total = lax.dot_general(gate_rows, d_gate, contract_outer, preferred_element_type=jnp.float32)
    summed = lax.psum_scatter(
        (
            total
            + lax.dot_general(up_rows, d_up, contract_outer, preferred_element_type=jnp.float32)
        ).astype(jnp.bfloat16),
        "tensor",
        scatter_dimension=0,
        tiled=True,
    ).astype(jnp.float32)
    slot_grad = summed.reshape(feature_share, groups, capacity)
    returned = lax.all_to_all(
        slot_grad.astype(jnp.bfloat16), "expert", split_axis=1, concat_axis=1, tiled=True
    ).astype(slot_grad.dtype)
    returned = returned.reshape(feature_share, assignments)
    grad_in = lax.dot_general(
        collect,
        returned,
        contract_inner,
        precision=lax.Precision.HIGHEST,
        preferred_element_type=jnp.float32,
    )
    return grad_in.astype(jnp.bfloat16)


def solution(mesh):
    placed = (
        P("expert", "tensor"),
        P("expert", None),
        P("expert", None),
        P("expert"),
        P("expert", "tensor", None),
        P("expert", "tensor", None),
        P("expert", "tensor", None),
        P("expert", None, "tensor", None),
    )
    return jax.shard_map(
        shards, mesh=mesh, in_specs=placed, out_specs=P("expert", "tensor"), check_vma=False
    )
```

profile of v0, /device:TPU:0, one launch (start us, length us, event | category | flops | bytes accessed | tf_op | source)
XLA Modules:
  0.0 254.3 jit_solution(9493166249357353603)
XLA Ops:
  6.5 0.0 all-gather.2.cloned.1.call-start
  6.5 0.8 copy.23
  7.3 0.1 eq.45
  7.4 0.1 eq.49
  7.5 0.7 broadcast_in_dim.16
  8.3 0.1 broadcast_in_dim.17
  8.4 0.1 broadcast_in_dim.18
  8.5 1.1 reduce-window.6
  9.6 0.2 slice_reduce_fusion
  9.9 0.7 broadcast_in_dim.19
  10.6 0.1 mul.58
  10.7 0.1 select_reduce_fusion
  10.9 0.0 copy-start.1
  10.9 2.9 %broadcast_in_dim.20 = f32[128,4,1024]{2,1,0:T(4,128)} broadcast(bf16[128,1024]{1,0:T(8,128)(2,1)} %param.8), dimensions={0,2} | broadcast | bytes 2359296 | tf_op jit(solution)/shard_map/broadcast_in_dim | solution.py:28
  13.7 2.0 convert_element_type.57
  15.7 0.0 copy-done.1
  15.7 0.1 copy.28
  15.8 0.1 mul.63
  15.9 0.9 convolution_convert_fusion
  16.8 20.4 %all_to_all.10 = bf16[8,64,1024]{2,1,0:T(8,128)(2,1)} all-to-all(bf16[8,64,1024]{2,1,0:T(8,128)(2,1)S(1)} %bitcast.48), channel_id=1, replica_groups=mesh['expert'=8,'tensor'=4] {'expert'}, dimensions={0} | all-to-all | bytes 2097152 | tf_op jit(solution)/shard_map/all_to_all | solution.py:33
  37.3 0.0 all-gather.2.cloned.1.call-update
  37.3 0.0 copy-start.2
  37.3 0.2 reduce-scatter.2.cloned.1.call-start
  37.5 80.0 %all-gather.2.cloned.1.call-done = bf16[512,4096]{1,0:T(8,128)(2,1)} async-done(((bf16[512,1024]{1,0:T(8,128)(2,1)}), bf16[512,4096]{1,0:T(8,128)(2,1)}) %all-gather.2.cloned.1.call-update) | async-done | bytes 4194320 | tf_op jit(solution)/shard_map/all_gather | solution.py:39
  117.6 0.0 slice-start
  117.6 0.0 slice-start.1
  117.6 10.1 %fusion.11 = f32[1344,512]{1,0:T(8,128)S(1)} fusion(bf16[512,4096]{1,0:T(8,128)(2,1)} %all-gather.2.cloned.1.call-done, bf16[1,1344,4096]{2,1,0:T(8,128)(2,1)} %param.14), kind=kOutput, calls=%fused_computation.11 | convolution fusion | flops 5637144576 | bytes 17956864 | tf_op jit(solution)/shard_map/dot_general | solution.py:37
  127.6 0.0 copy-done.2
  127.6 0.0 slice-start.2
  127.7 11.9 %fusion = f32[512,4096]{1,0:T(8,128)} fusion(bf16[1,1344,4096]{2,1,0:T(8,128)(2,1)} %param.13, f32[1344,512]{1,0:T(8,128)S(1)} %fusion.11, bf16[1,2,1344,512]{3,2,1,0:T(8,128)(2,1)S(1)} %copy-done.2), kind=kOutput, calls=%fused_computation | convolution fusion | flops 5641961472 | bytes 23527424 | tf_op jit(solution)/shard_map/dot_general | solution.py:58
  139.5 0.0 slice-done
  139.5 0.0 slice-done.1
  139.5 0.0 slice-done.2
  139.6 12.1 %fusion.8 = bf16[4096,512]{0,1:T(8,128)(2,1)} fusion(f32[512,4096]{1,0:T(8,128)} %fusion, bf16[1,1344,4096]{2,1,0:T(8,128)(2,1)S(1)} %bitcast.51, f32[1344,512]{1,0:T(8,128)S(1)} %fusion.11, bf16[1,2,1344,512]{3,2,1,0:T(8,128)(2,1)S(1)} %copy-done.2), kind=kOutput, calls=%fused_computation.7 | convolution fusion | flops 5649596416 | bytes 29097984 | tf_op jit(solution)/shard_map/dot_general | solution.py:54
  151.7 0.0 copy-start
  151.7 0.0 reduce-scatter.2.cloned.1.call-update
  151.7 75.4 %reduce-scatter.2.cloned.1.call-done = bf16[1024,512]{0,1:T(8,128)(2,1)} async-done(((bf16[4096,512]{0,1:T(8,128)(2,1)}), bf16[1024,512]{0,1:T(8,128)(2,1)}) %reduce-scatter.2.cloned.1.call-update) | async-done | bytes 1048592 | tf_op jit(solution)/shard_map/reduce_scatter | solution.py:55
  227.1 3.7 %all-to-all-start.1 = ((bf16[1024,8,64]{0,2,1:T(8,128)(2,1)}), bf16[1024,8,64]{0,2,1:T(8,128)(2,1)S(1)}, u32[]{:S(2)}, u32[]{:S(2)}) async-start(bf16[1024,8,64]{0,2,1:T(8,128)(2,1)} %bitcast.49), calls=%async_computation.2 | async-start | bytes 2097152 | tf_op jit(solution)/shard_map/all_to_all | solution.py:65
  230.8 0.1 reduce_sum.30
  230.9 0.1 gt.16
  231.0 0.1 copy.27
  231.1 0.1 copy.25
  231.2 0.0 copy-done
  231.2 0.2 convert_reduce_fusion
  231.5 14.7 %all-to-all-done.1 = bf16[1024,8,64]{0,2,1:T(8,128)(2,1)S(1)} async-done(((bf16[1024,8,64]{0,2,1:T(8,128)(2,1)}), bf16[1024,8,64]{0,2,1:T(8,128)(2,1)S(1)}, u32[]{:S(2)}, u32[]{:S(2)}) %all-to-all-start.1) | async-done | bytes 1048608 | tf_op jit(solution)/shard_map/all_to_all | solution.py:65
  246.2 1.3 convolution_convert_fusion.1
  (8 shorter events, 0.1 us)
Async XLA Ops:
  6.5 111.0 %all-gather.2.cloned.1.call-start = ((), (), s32[]{:S(2)}) async-start(), calls=%async_computation.3 | async-start | bytes 5242880 | tf_op jit(solution)/shard_map/all_gather | solution.py:39
  10.9 4.9 %copy-start.1 = (f32[128,4]{0,1:T(4,128)S(1)}, f32[128,4]{0,1:T(4,128)}, u32[]{:S(2)}) copy-start(f32[128,4]{0,1:T(4,128)} %param.10) | copy-start | bytes 6148
  37.3 90.3 %copy-start.2 = (bf16[1,2,1344,512]{3,2,1,0:T(8,128)(2,1)S(1)}, bf16[1,2,1344,512]{3,2,1,0:T(8,128)(2,1)}, u32[]{:S(2)}) copy-start(bf16[1,2,1344,512]{3,2,1,0:T(8,128)(2,1)} %param.15) | copy-start | bytes 8257540
  37.3 189.8 %reduce-scatter.2.cloned.1.call-start = ((), (), s32[]{:S(2)}) async-start(), calls=%async_computation.4 | async-start | bytes 5242880 | tf_op jit(solution)/shard_map/reduce_scatter | solution.py:55
  117.6 22.0 %slice-start = ((s8[11010048]{0:T(1024)(128)(4,1)}), s8[4194304]{0:T(1024)(128)(4,1)S(1)}, s32[]{:S(2)}) async-start(s8[11010048]{0:T(1024)(128)(4,1)} %bitcast.50), calls=%async_computation.5 | async-start | bytes 8388608
  117.6 22.0 %slice-start.1 = ((s8[11010048]{0:T(1024)(128)(4,1)}), s8[4194304]{0:T(1024)(128)(4,1)S(1)}, s32[]{:S(2)}) async-start(s8[11010048]{0:T(1024)(128)(4,1)} %bitcast.50), calls=%async_computation.6 | async-start | bytes 8388608
  127.6 11.9 %slice-start.2 = ((s8[11010048]{0:T(1024)(128)(4,1)}), s8[2621440]{0:T(1024)(128)(4,1)S(1)}, s32[]{:S(2)}) async-start(s8[11010048]{0:T(1024)(128)(4,1)} %bitcast.50), calls=%async_computation.7 | async-start | bytes 5242880
  151.7 79.5 %copy-start = (s32[128,4]{0,1:T(4,128)S(1)}, s32[128,4]{0,1:T(4,128)}, u32[]{:S(2)}) copy-start(s32[128,4]{0,1:T(4,128)} %param.9) | copy-start | bytes 6148
  227.1 19.0 %all-to-all-start.1 = ((bf16[1024,8,64]{0,2,1:T(8,128)(2,1)}), bf16[1024,8,64]{0,2,1:T(8,128)(2,1)S(1)}, u32[]{:S(2)}, u32[]{:S(2)}) async-start(bf16[1024,8,64]{0,2,1:T(8,128)(2,1)} %bitcast.49), calls=%async_computation.2 | async-start | bytes 2097152 | tf_op jit(solution)/shard_map/all_to_all | solution.py:65
Sparse Core Ops, SparseCore 0:
  37.4 80.0 all-gather.1
  151.8 75.2 reduce-scatter.1
where the time goes:
time: 255 us; the launch traced here: 254 us
  waiting for transfers between devices  170 us (67%)
  matrix products  36.2 us (14%)
  blocking collectives  20.4 us (8%)
  between operations  13.5 us (5%)
  local copies, waits for them, and re-layouts  8.48 us (3%)
  starting transfers between devices  3.88 us (2%)
    all_gather x1, waiting for transfers between devices, shards(): lax.all_gather(arrived, 'tensor', axis=1, tiled=True)  80 us
    reduce_scatter x1, waiting for transfers between devices, shards(): lax.psum_scatter((total + lax.dot_general(up_rows, d_up, contract_outer,...  75.4 us
    all_to_all x1, blocking collectives, shards(): lax.all_to_all(outgoing.reshape(groups, capacity, -1), 'expert', split_ax...  20.4 us
    all_to_all x1, waiting for transfers between devices, shards(): lax.all_to_all(slot_grad.astype(jnp.bfloat16), 'expert', split_axis=1, co...  14.7 us
    dot_general x1, matrix products, shards(): lax.dot_general(gate_rows, d_gate, contract_outer, preferred_element_type...  12.1 us
    dot_general x1, matrix products, shards(): lax.dot_general(up_rows, d_up, contract_outer, preferred_element_type=jnp...  11.9 us
    dot_general x1, matrix products, shards(): lax.dot_general(down_rows, lax.all_gather(arrived, 'tensor', axis=1, tile...  10.1 us
  transfers between devices with their start and end apart: 3, of which 3 were waited for; matrix products, arithmetic and copies ran while one was open for 0% of the time, Pallas kernels for 0%

commit v1 on v0

v1 whole, which is shorter than its diff:
```python
import functools

import jax
import jax.numpy as jnp
from jax import lax
from jax.experimental import pallas as pl
from jax.experimental.pallas import tpu as pltpu
from jax.sharding import PartitionSpec as P

MESH = pl.DeviceIdType.MESH
NT = (((1,), (1,)), ((), ()))
NN = (((1,), (0,)), ((), ()))


def dot(a, b, dims):
    return lax.dot_general(a, b, dims, preferred_element_type=jnp.float32)


def mate(me, step, size, sign):
    if size & (size - 1):
        return lax.rem(me + (sign * step) % size, size)
    out, bit = 0, 1
    while bit < size:
        mine = lax.rem(lax.div(me, bit), 2)
        out = out + (1 - mine if step & bit else mine) * bit
        bit *= 2
    return out


def kernel(
    ne, nt, cap, raw0, ids, gates, live, w_gate, w_up, w_down, saved, out,
    wd, wg, wu, sv, svt, dh, sel, gs, back, outgoing, recv, orecv, raw, part, zrecv,
    w_sem, sv_sem, in_send, in_recv, out_send, out_recv, z_send, z_recv, p_send, p_recv,
):
    me = lax.axis_index("expert")
    mz = lax.axis_index("tensor")
    tokens, chunk = raw0.shape
    slots = ne * cap
    hidden = saved.shape[2]
    tops = ids.shape[0]
    steps = range(nt)
    owner = [mate(mz, s, nt, 1) for s in steps]
    zpeer = [mate(mz, s, nt, -1) for s in steps]
    order = sorted(range(1, ne), key=lambda j: (-(j // 2) if j > 1 else 1, j))
    epeer = [mate(me, j, ne, 1) for j in order]

    barrier = pltpu.get_barrier_semaphore()
    for peer in epeer:
        pl.semaphore_signal(barrier, inc=1, device_id=(peer, mz), device_id_type=MESH)
    for s in range(1, nt):
        pl.semaphore_signal(barrier, inc=1, device_id=(me, zpeer[s]), device_id_type=MESH)

    def weight_copy(i, s):
        src = (w_down, w_gate, w_up)[i]
        dst = (wd, wg, wu)[i]
        columns = pl.ds(pl.multiple_of(owner[s] * chunk, chunk), chunk)
        return pltpu.make_async_copy(src.at[0, :, columns], dst.at[s], w_sem.at[i, s])

    saved_copy = pltpu.make_async_copy(saved.at[0], sv, sv_sem.at[0])

    experts = lax.broadcasted_iota(jnp.int32, (ne, tokens), 0)
    alive = live[...] != 0
    chosen = jnp.zeros((ne, tokens), jnp.float32)
    weight = jnp.zeros((ne, tokens), jnp.float32)
    for k in range(tops):
        match = (ids[k : k + 1, :] == experts) & alive
        chosen = chosen + jnp.where(match, 1.0, 0.0)
        weight = weight + jnp.where(match, gates[k : k + 1, :], 0.0)
    row = lax.broadcasted_iota(jnp.int32, (tokens, tokens), 0)
    col = lax.broadcasted_iota(jnp.int32, (tokens, tokens), 1)
    before = jnp.where(row < col, 1.0, 0.0).astype(jnp.bfloat16)
    position = dot(chosen.astype(jnp.bfloat16), before, NN)
    position = jnp.where((chosen > 0.0) & (position < cap), position, -1.0)
    slot = lax.broadcasted_iota(jnp.int32, (cap, tokens), 0).astype(jnp.float32)
    for e in range(ne):
        hit = slot == position[e : e + 1, :]
        sel[e * cap : (e + 1) * cap, :] = jnp.where(hit, 1.0, 0.0).astype(jnp.bfloat16)
        gate = jnp.sum(jnp.where(hit, weight[e : e + 1, :], 0.0), axis=1, keepdims=True)
        gs[e * cap : (e + 1) * cap, :] = jnp.broadcast_to(gate, (cap, gs.shape[1]))

    tile = min(256, chunk)

    def build(src, s):
        @pl.loop(0, chunk // tile)
        def _(c):
            columns = pl.ds(pl.multiple_of(c * tile, tile), tile)
            picked = dot(sel[...], src[:, columns], NN)
            outgoing[s, :, columns] = (gs[:, :1] * picked).astype(jnp.bfloat16)

    def rows(e):
        return pl.ds(pl.multiple_of(e * cap, cap), cap)

    def exchange(s, dst, send, receive):
        for peer in epeer:
            pltpu.make_async_remote_copy(
                src_ref=outgoing.at[s, rows(peer)],
                dst_ref=dst.at[s, rows(me)],
                send_sem=send.at[s],
                recv_sem=receive.at[s],
                device_id=(peer, mz),
                device_id_type=MESH,
            ).start()
        pltpu.make_async_copy(
            outgoing.at[s, rows(me)], dst.at[s, rows(me)], receive.at[s]
        ).start()

    def wait_all(ref, sem):
        pltpu.make_async_copy(ref, ref, sem).wait()

    def z_copy(src, dst, s, send, receive, peer):
        return pltpu.make_async_remote_copy(
            src_ref=src,
            dst_ref=dst,
            send_sem=send.at[s],
            recv_sem=receive.at[s],
            device_id=(me, peer),
            device_id_type=MESH,
        )

    build(raw0, 0)
    pl.semaphore_wait(barrier, ne - 1 + nt - 1)
    z_copies = [
        z_copy(raw0, raw.at[s], s, z_send, z_recv, zpeer[s]) for s in range(1, nt)
    ]
    for copy in z_copies:
        copy.start()
    exchange(0, recv, in_send, in_recv)

    saved_copy.start()
    for s in steps:
        weight_copy(0, s).start()
    for s in reversed(steps):
        weight_copy(1, s).start()
        weight_copy(2, s).start()

    for s in range(1, nt):
        z_copies[s - 1].wait_recv()
        build(raw.at[s], s)
        exchange(s, recv, in_send, in_recv)

    row = lax.broadcasted_iota(jnp.int32, (tokens, tokens), 0)
    col = lax.broadcasted_iota(jnp.int32, (tokens, tokens), 1)
    eye = jnp.where(row == col, 1.0, 0.0).astype(jnp.bfloat16)
    back[...] = dot(eye, sel[...], NT).astype(jnp.bfloat16)
    block = min(128, slots)
    saved_copy.wait()

    @pl.loop(0, slots // block)
    def _(b):
        at = pl.ds(pl.multiple_of(b * block, block), block)
        r = lax.broadcasted_iota(jnp.int32, (block, block), 0)
        c = lax.broadcasted_iota(jnp.int32, (block, block), 1)
        one = jnp.where(r == c, 1.0, 0.0).astype(jnp.bfloat16)
        for i in range(2):
            svt[i, at, :] = dot(one, sv[i, :, at], NT).astype(jnp.bfloat16)

    half = min(256, slots)
    for s in steps:
        weight_copy(0, s).wait()
        wait_all(recv.at[s], in_recv.at[s])

        @pl.loop(0, slots // half)
        def _(b):
            at = pl.ds(pl.multiple_of(b * half, half), half)
            part_sum = dot(recv[s, at, :], wd[s], NT)
            if s == 0:
                dh[at, :] = part_sum
            else:
                dh[at, :] = dh[at, :] + part_sum

    few = 16

    @pl.loop(0, slots // few)
    def _(b):
        at = pl.ds(pl.multiple_of(b * few, few), few)
        grad = dh[at, :]
        a = svt[0, at, :].astype(jnp.float32)
        u = svt[1, at, :].astype(jnp.float32)
        sig = jax.nn.sigmoid(a)
        svt[1, at, :] = (grad * a * sig).astype(jnp.bfloat16)
        svt[0, at, :] = (grad * u * sig * (1.0 + a * (1.0 - sig))).astype(jnp.bfloat16)

    def combine(s, columns):
        return dot(back[...], orecv[s, :, columns], NN)

    p_copies = {
        s: z_copy(part.at[s], zrecv.at[s], s, p_send, p_recv, owner[s])
        for s in range(1, nt)
    }

    def finish(s):
        wait_all(orecv.at[s], out_recv.at[s])
        if s == 0:
            for q in range(1, nt):
                p_copies[q].wait_recv()

        @pl.loop(0, chunk // tile)
        def _(c):
            columns = pl.ds(pl.multiple_of(c * tile, tile), tile)
            total = combine(s, columns)
            if s == 0:
                for q in range(1, nt):
                    total = total + zrecv[q, :, columns].astype(jnp.float32)
                out[:, columns] = total.astype(jnp.bfloat16)
            else:
                part[s, :, columns] = total.astype(jnp.bfloat16)

        if s > 0:
            p_copies[s].start()

    others = outgoing.at[0, pl.ds(0, (ne - 1) * cap)]
    for s in reversed(steps):
        wait_all(others, in_send.at[s])
        weight_copy(1, s).wait()
        weight_copy(2, s).wait()

        @pl.loop(0, chunk // tile)
        def _(c):
            columns = pl.ds(pl.multiple_of(c * tile, tile), tile)
            term = dot(svt[0], wg[s, :, columns], NN)
            term = term + dot(svt[1], wu[s, :, columns], NN)
            outgoing[s, :, columns] = term.astype(jnp.bfloat16)

        exchange(s, orecv, out_send, out_recv)
    for s in reversed(steps):
        finish(s)

    for s in steps:
        wait_all(others, out_send.at[s])
    for s in range(1, nt):
        z_copies[s - 1].wait_send()
        p_copies[s].wait_send()


def shards(grad_out, expert_ids, gate_probs, live, w_gate, w_up, w_down, saved):
    ne = lax.axis_size("expert")
    nt = lax.axis_size("tensor")
    tokens, chunk = grad_out.shape
    cap = tokens * expert_ids.shape[1] // ne
    slots = ne * cap
    hidden = saved.shape[2]
    bf16, f32 = jnp.bfloat16, jnp.float32
    vmem = pl.BlockSpec(memory_space=pltpu.VMEM)
    anywhere = pl.BlockSpec(memory_space=pl.ANY)
    dma = pltpu.SemaphoreType.DMA
    return pl.pallas_call(
        functools.partial(kernel, ne, nt, cap),
        out_shape=jax.ShapeDtypeStruct((tokens, chunk), bf16),
        in_specs=[vmem] * 4 + [anywhere] * 4,
        out_specs=vmem,
        scratch_shapes=[
            pltpu.VMEM((nt, hidden, chunk), bf16),
            pltpu.VMEM((nt, hidden, chunk), bf16),
            pltpu.VMEM((nt, hidden, chunk), bf16),
            pltpu.VMEM((2, hidden, slots), bf16),
            pltpu.VMEM((2, slots, hidden), bf16),
            pltpu.VMEM((slots, hidden), f32),
            pltpu.VMEM((slots, tokens), bf16),
            pltpu.VMEM((slots, 128), f32),
            pltpu.VMEM((tokens, slots), bf16),
            pltpu.VMEM((nt, slots, chunk), bf16),
            pltpu.VMEM((nt, slots, chunk), bf16),
            pltpu.VMEM((nt, slots, chunk), bf16),
            pltpu.VMEM((nt, tokens, chunk), bf16),
            pltpu.VMEM((nt, tokens, chunk), bf16),
            pltpu.VMEM((nt, tokens, chunk), bf16),
            dma((3, nt)),
            dma((1,)),
            dma((nt,)),
            dma((nt,)),
            dma((nt,)),
            dma((nt,)),
            dma((nt,)),
            dma((nt,)),
            dma((nt,)),
            dma((nt,)),
        ],
        compiler_params=pltpu.CompilerParams(
            collective_id=0, has_side_effects=True, vmem_limit_bytes=67043328
        ),
    )(
        grad_out,
        expert_ids.T,
        gate_probs.T,
        live.reshape(1, tokens),
        w_gate,
        w_up,
        w_down,
        saved,
    )


def solution(mesh):
    placed = (
        P("expert", "tensor"),
        P("expert", None),
        P("expert", None),
        P("expert"),
        P("expert", "tensor", None),
        P("expert", "tensor", None),
        P("expert", "tensor", None),
        P("expert", None, "tensor", None),
    )
    return jax.shard_map(
        shards, mesh=mesh, in_specs=placed, out_specs=P("expert", "tensor"), check_vma=False
    )
```

time: 255 us -> 113 us (0.44)
  waiting for transfers between devices: 170 us -> 0 us
  Pallas kernels: 0 us -> 111 us
  matrix products: 36.2 us -> 0 us
  blocking collectives: 20.4 us -> 0 us
  between operations: 13.5 us -> 0.01 us
  local copies, waits for them, and re-layouts: 8.48 us -> 1.67 us
  starting transfers between devices: 3.88 us -> 0 us
    pallas_call x0 -> x1, Pallas kernels: none -> 111 us  [shards(): pl.pallas_call(functools.partial(kernel, ne, nt, cap), out_shape=jax.Shap...]
    all_gather x1 -> x0, waiting for transfers between devices: 80 us -> none  [shards(): lax.all_gather(arrived, 'tensor', axis=1, tiled=True)]
    reduce_scatter x1 -> x0, waiting for transfers between devices: 75.4 us -> none  [shards(): lax.psum_scatter((total + lax.dot_general(up_rows, d_up, contract_outer,...]
    dot_general x5 -> x0, matrix products: 36.2 us -> none  [the longest x1 12.1 us: shards(): lax.dot_general(gate_rows, d_gate, contract_outer, preferred_element_type...]
    all_to_all x1 -> x0, blocking collectives: 20.4 us -> none  [shards(): lax.all_to_all(outgoing.reshape(groups, capacity, -1), 'expert', split_ax...]
    all_to_all x1 -> x0, waiting for transfers between devices: 14.7 us -> none  [shards(): lax.all_to_all(slot_grad.astype(jnp.bfloat16), 'expert', split_axis=1, co...]
    broadcast_in_dim x5 -> x0, local copies, waits for them, and re-layouts: 4.53 us -> none  [the longest x1 2.86 us: shards(): repeated = jnp.repeat(grad_out, top_count, axis=0)]
    all_to_all x1 -> x0, starting transfers between devices: 3.65 us -> none  [shards(): lax.all_to_all(slot_grad.astype(jnp.bfloat16), 'expert', split_axis=1, co...]
  transfers between devices with their start and end apart: 3 -> 0, of which waited for: 3 -> 0; matrix products, arithmetic and copies ran while one was open for 0% -> 0% of each run, Pallas kernels for 0% -> 0%
where the time goes in v1:
time: 113 us
  Pallas kernels  111 us (98%)
  local copies, waits for them, and re-layouts  1.67 us (1%)
    pallas_call x1, Pallas kernels, shards(): pl.pallas_call(functools.partial(kernel, ne, nt, cap), out_shape=jax.Shap...  111 us

profile of v1, /device:TPU:0, one launch (start us, length us, event | category | flops | bytes accessed | tf_op | source)
XLA Modules:
  0.0 113.1 jit_solution(11197897355123632137)
XLA Ops:
  0.0 111.4 %shard_map.82 = bf16[128,1024]{1,0:T(8,128)(2,1)} custom-call(bf16[128,1024]{1,0:T(8,128)(2,1)} %raw0.1, s32[4,128]{1,0:T(4,128)} %bitcast.3, f32[4,128]{1,0:T(4,128)} %bitcast.4, s32[1,128]{1,0:T(1,128)} %bitcast.5, bf16[1,1344,4096]{2,1,0:T(8,128)(2,1)} %w_gate.1, bf16[1,1344,4096]{2,1,0:T(8,128)(2,1)} %w_up.1, bf16[1,1344,4096]{2,1,0:T(8,128)(2,1)} %w_down.1, ...), custom_call_target="tpu_custom_call" | custom-call | tf_op jit(solution)/shard_map/pallas_call | solution.py:246
  111.4 1.7 %copy.10 = bf16[128,1024]{1,0:T(8,128)(2,1)} copy(bf16[128,1024]{1,0:T(8,128)(2,1)} %shard_map.82) | data formatting | bytes 524288

commit v2 on v1

--- a/solution.py
+++ b/solution.py
@@ -10,6 +10,7 @@
 MESH = pl.DeviceIdType.MESH
 NT = (((1,), (1,)), ((), ()))
 NN = (((1,), (0,)), ((), ()))
+PARTS = 2
 
 
 def dot(a, b, dims):
@@ -35,8 +36,8 @@
     me = lax.axis_index("expert")
     mz = lax.axis_index("tensor")
     tokens, chunk = raw0.shape
-    slots = ne * cap
-    hidden = saved.shape[2]
+    few = cap // PARTS
+    slots = ne * few
     tops = ids.shape[0]
     steps = range(nt)
     owner = [mate(mz, s, nt, 1) for s in steps]
@@ -71,24 +72,26 @@
     before = jnp.where(row < col, 1.0, 0.0).astype(jnp.bfloat16)
     position = dot(chosen.astype(jnp.bfloat16), before, NN)
     position = jnp.where((chosen > 0.0) & (position < cap), position, -1.0)
-    slot = lax.broadcasted_iota(jnp.int32, (cap, tokens), 0).astype(jnp.float32)
-    for e in range(ne):
-        hit = slot == position[e : e + 1, :]
-        sel[e * cap : (e + 1) * cap, :] = jnp.where(hit, 1.0, 0.0).astype(jnp.bfloat16)
-        gate = jnp.sum(jnp.where(hit, weight[e : e + 1, :], 0.0), axis=1, keepdims=True)
-        gs[e * cap : (e + 1) * cap, :] = jnp.broadcast_to(gate, (cap, gs.shape[1]))
+    slot = lax.broadcasted_iota(jnp.int32, (few, tokens), 0).astype(jnp.float32)
+    for h in range(PARTS):
+        for e in range(ne):
+            at = slice(e * few, (e + 1) * few)
+            hit = slot + float(h * few) == position[e : e + 1, :]
+            sel[h, at, :] = jnp.where(hit, 1.0, 0.0).astype(jnp.bfloat16)
+            gate = jnp.sum(jnp.where(hit, weight[e : e + 1, :], 0.0), axis=1, keepdims=True)
+            gs[h, at, :] = jnp.broadcast_to(gate, (few, gs.shape[2]))
 
     tile = min(256, chunk)
 
-    def build(src, s):
+    def build(src, h, s):
         @pl.loop(0, chunk // tile)
         def _(c):
             columns = pl.ds(pl.multiple_of(c * tile, tile), tile)
-            picked = dot(sel[...], src[:, columns], NN)
-            outgoing[s, :, columns] = (gs[:, :1] * picked).astype(jnp.bfloat16)
+            picked = dot(sel[h], src[:, columns], NN)
+            outgoing[h * nt + s, :, columns] = (gs[h, :, :1] * picked).astype(jnp.bfloat16)
 
     def rows(e):
-        return pl.ds(pl.multiple_of(e * cap, cap), cap)
+        return pl.ds(pl.multiple_of(e * few, few), few)
 
     def exchange(s, dst, send, receive):
         for peer in epeer:
@@ -117,7 +120,7 @@
             device_id_type=MESH,
         )
 
-    build(raw0, 0)
+    build(raw0, 0, 0)
     pl.semaphore_wait(barrier, ne - 1 + nt - 1)
     z_copies = [
         z_copy(raw0, raw.at[s], s, z_send, z_recv, zpeer[s]) for s in range(1, nt)
@@ -133,55 +136,87 @@
         weight_copy(1, s).start()
         weight_copy(2, s).start()
 
-    for s in range(1, nt):
-        z_copies[s - 1].wait_recv()
-        build(raw.at[s], s)
-        exchange(s, recv, in_send, in_recv)
+    def transpose_saved():
+        saved_copy.wait()
+        block = min(128, slots)
+        for h in range(PARTS):
+
+            @pl.loop(0, slots // block)
+            def _(b):
+                r = lax.broadcasted_iota(jnp.int32, (block, ne * cap), 0) + b * block
+                c = lax.broadcasted_iota(jnp.int32, (block, ne * cap), 1)
+                r = r.astype(jnp.float32)
+                group = jnp.floor((r + 0.5) * (1.0 / few))
+                place = r + group * float(cap - few) + float(h * few)
+                one = jnp.where(place == c.astype(jnp.float32), 1.0, 0.0).astype(jnp.bfloat16)
+                at = pl.ds(pl.multiple_of(b * block, block), block)
+                for i in range(2):
+                    svt[h, i, at, :] = dot(one, sv[i], NT).astype(jnp.bfloat16)
+
+    units = [(0, s) for s in range(1, nt)] + [(h, s) for h in range(1, PARTS) for s in steps]
+    if nt > 1:
+        units.remove((1, 0))
+        units.insert(1, (1, 0))
+    for number, (h, s) in enumerate(units):
+        if s > 0 and h == 0:
+            z_copies[s - 1].wait_recv()
+        build(raw.at[s] if s > 0 else raw0, h, s)
+        exchange(h * nt + s, recv, in_send, in_recv)
+        if number == 1:
+            transpose_saved()
 
     row = lax.broadcasted_iota(jnp.int32, (tokens, tokens), 0)
     col = lax.broadcasted_iota(jnp.int32, (tokens, tokens), 1)
     eye = jnp.where(row == col, 1.0, 0.0).astype(jnp.bfloat16)
-    back[...] = dot(eye, sel[...], NT).astype(jnp.bfloat16)
-    block = min(128, slots)
-    saved_copy.wait()
-
-    @pl.loop(0, slots // block)
-    def _(b):
-        at = pl.ds(pl.multiple_of(b * block, block), block)
-        r = lax.broadcasted_iota(jnp.int32, (block, block), 0)
-        c = lax.broadcasted_iota(jnp.int32, (block, block), 1)
-        one = jnp.where(r == c, 1.0, 0.0).astype(jnp.bfloat16)
-        for i in range(2):
-            svt[i, at, :] = dot(one, sv[i, :, at], NT).astype(jnp.bfloat16)
-
-    half = min(256, slots)
-    for s in steps:
-        weight_copy(0, s).wait()
-        wait_all(recv.at[s], in_recv.at[s])
-
-        @pl.loop(0, slots // half)
+    for h in range(PARTS):
+        back[h] = dot(eye, sel[h], NT).astype(jnp.bfloat16)
+
+    others = outgoing.at[0, pl.ds(0, (ne - 1) * few)]
+
+    def hidden_gradients(h):
+        for s in steps:
+            if h == 0:
+                weight_copy(0, s).wait()
+            wait_all(recv.at[h * nt + s], in_recv.at[h * nt + s])
+            share = dot(recv[h * nt + s], wd[s], NT)
+            if s == 0:
+                dh[...] = share
+            else:
+                dh[...] = dh[...] + share
+
+        thin = 16
+
+        @pl.loop(0, slots // thin)
         def _(b):
-            at = pl.ds(pl.multiple_of(b * half, half), half)
-            part_sum = dot(recv[s, at, :], wd[s], NT)
-            if s == 0:
-                dh[at, :] = part_sum
-            else:
-                dh[at, :] = dh[at, :] + part_sum
-
-    few = 16
-
-    @pl.loop(0, slots // few)
-    def _(b):
-        at = pl.ds(pl.multiple_of(b * few, few), few)
-        grad = dh[at, :]
-        a = svt[0, at, :].astype(jnp.float32)
-        u = svt[1, at, :].astype(jnp.float32)
-        sig = jax.nn.sigmoid(a)
-        svt[1, at, :] = (grad * a * sig).astype(jnp.bfloat16)
-        svt[0, at, :] = (grad * u * sig * (1.0 + a * (1.0 - sig))).astype(jnp.bfloat16)
+            at = pl.ds(pl.multiple_of(b * thin, thin), thin)
+            grad = dh[at, :]
+            a = svt[h, 0, at, :].astype(jnp.float32)
+            u = svt[h, 1, at, :].astype(jnp.float32)
+            sig = jax.nn.sigmoid(a)
+            svt[h, 1, at, :] = (grad * a * sig).astype(jnp.bfloat16)
+            svt[h, 0, at, :] = (grad * u * sig * (1.0 + a * (1.0 - sig))).astype(jnp.bfloat16)
+
+    def terms(h, s):
+        unit = h * nt + s
+        wait_all(others, in_send.at[unit])
+        if h == 0:
+            weight_copy(1, s).wait()
+            weight_copy(2, s).wait()
+
+        @pl.loop(0, chunk // tile)
+        def _(c):
+            columns = pl.ds(pl.multiple_of(c * tile, tile), tile)
+            term = dot(svt[h, 0], wg[s, :, columns], NN)
+            term = term + dot(svt[h, 1], wu[s, :, columns], NN)
+            outgoing[unit, :, columns] = term.astype(jnp.bfloat16)
+
+        exchange(unit, orecv, out_send, out_recv)
 
     def combine(s, columns):
-        return dot(back[...], orecv[s, :, columns], NN)
+        total = dot(back[0], orecv[s, :, columns], NN)
+        for h in range(1, PARTS):
+            total = total + dot(back[h], orecv[h * nt + s, :, columns], NN)
+        return total
 
     p_copies = {
         s: z_copy(part.at[s], zrecv.at[s], s, p_send, p_recv, owner[s])
@@ -189,7 +224,8 @@
     }
 
     def finish(s):
-        wait_all(orecv.at[s], out_recv.at[s])
+        for h in range(PARTS):
+            wait_all(orecv.at[h * nt + s], out_recv.at[h * nt + s])
         if s == 0:
             for q in range(1, nt):
                 p_copies[q].wait_recv()
@@ -208,25 +244,15 @@
         if s > 0:
             p_copies[s].start()
 
-    others = outgoing.at[0, pl.ds(0, (ne - 1) * cap)]
-    for s in reversed(steps):
-        wait_all(others, in_send.at[s])
-        weight_copy(1, s).wait()
-        weight_copy(2, s).wait()
-
-        @pl.loop(0, chunk // tile)
-        def _(c):
-            columns = pl.ds(pl.multiple_of(c * tile, tile), tile)
-            term = dot(svt[0], wg[s, :, columns], NN)
-            term = term + dot(svt[1], wu[s, :, columns], NN)
-            outgoing[s, :, columns] = term.astype(jnp.bfloat16)
-
-        exchange(s, orecv, out_send, out_recv)
+    for h in range(PARTS):
+        hidden_gradients(h)
+        for s in reversed(steps):
+            terms(h, s)
     for s in reversed(steps):
         finish(s)
 
-    for s in steps:
-        wait_all(others, out_send.at[s])
+    for unit in range(PARTS * nt):
+        wait_all(others, out_send.at[unit])
     for s in range(1, nt):
         z_copies[s - 1].wait_send()
         p_copies[s].wait_send()
@@ -238,6 +264,7 @@
     tokens, chunk = grad_out.shape
     cap = tokens * expert_ids.shape[1] // ne
     slots = ne * cap
+    part_slots = slots // PARTS
     hidden = saved.shape[2]
     bf16, f32 = jnp.bfloat16, jnp.float32
     vmem = pl.BlockSpec(memory_space=pltpu.VMEM)
@@ -253,23 +280,23 @@
             pltpu.VMEM((nt, hidden, chunk), bf16),
             pltpu.VMEM((nt, hidden, chunk), bf16),
             pltpu.VMEM((2, hidden, slots), bf16),
-            pltpu.VMEM((2, slots, hidden), bf16),
-            pltpu.VMEM((slots, hidden), f32),
-            pltpu.VMEM((slots, tokens), bf16),
-            pltpu.VMEM((slots, 128), f32),
-            pltpu.VMEM((tokens, slots), bf16),
-            pltpu.VMEM((nt, slots, chunk), bf16),
-            pltpu.VMEM((nt, slots, chunk), bf16),
-            pltpu.VMEM((nt, slots, chunk), bf16),
+            pltpu.VMEM((PARTS, 2, part_slots, hidden), bf16),
+            pltpu.VMEM((part_slots, hidden), f32),
+            pltpu.VMEM((PARTS, part_slots, tokens), bf16),
+            pltpu.VMEM((PARTS, part_slots, 128), f32),
+            pltpu.VMEM((PARTS, tokens, part_slots), bf16),
+            pltpu.VMEM((PARTS * nt, part_slots, chunk), bf16),
+            pltpu.VMEM((PARTS * nt, part_slots, chunk), bf16),
+            pltpu.VMEM((PARTS * nt, part_slots, chunk), bf16),
             pltpu.VMEM((nt, tokens, chunk), bf16),
             pltpu.VMEM((nt, tokens, chunk), bf16),
             pltpu.VMEM((nt, tokens, chunk), bf16),
             dma((3, nt)),
             dma((1,)),
-            dma((nt,)),
-            dma((nt,)),
-            dma((nt,)),
-            dma((nt,)),
+            dma((PARTS * nt,)),
+            dma((PARTS * nt,)),
+            dma((PARTS * nt,)),
+            dma((PARTS * nt,)),
             dma((nt,)),
             dma((nt,)),
             dma((nt,)),

time: 113 us -> 114 us (level)
  no operation moved by 1% of the time
where the time goes in v2:
time: 114 us; the launch traced here: 113 us
  Pallas kernels  112 us (98%)
  local copies, waits for them, and re-layouts  1.67 us (1%)
    pallas_call x1, Pallas kernels, shards(): pl.pallas_call(functools.partial(kernel, ne, nt, cap), out_shape=jax.Shap...  112 us

profile of v2, /device:TPU:0, one launch (start us, length us, event | category | flops | bytes accessed | tf_op | source)
XLA Modules:
  0.0 113.5 jit_solution(8582163193577986967)
XLA Ops:
  0.0 111.8 %shard_map.82 = bf16[128,1024]{1,0:T(8,128)(2,1)} custom-call(bf16[128,1024]{1,0:T(8,128)(2,1)} %raw0.1, s32[4,128]{1,0:T(4,128)} %bitcast.3, f32[4,128]{1,0:T(4,128)} %bitcast.4, s32[1,128]{1,0:T(1,128)} %bitcast.5, bf16[1,1344,4096]{2,1,0:T(8,128)(2,1)} %w_gate.1, bf16[1,1344,4096]{2,1,0:T(8,128)(2,1)} %w_up.1, bf16[1,1344,4096]{2,1,0:T(8,128)(2,1)} %w_down.1, ...), custom_call_target="tpu_custom_call" | custom-call | tf_op jit(solution)/shard_map/pallas_call | solution.py:273
  111.8 1.7 %copy.10 = bf16[128,1024]{1,0:T(8,128)(2,1)} copy(bf16[128,1024]{1,0:T(8,128)(2,1)} %shard_map.82) | data formatting | bytes 524288

commit v3 on v1

--- a/solution.py
+++ b/solution.py
@@ -25,6 +25,10 @@
         out = out + (1 - mine if step & bit else mine) * bit
         bit *= 2
     return out
+
+
+def pieces_of(chunk):
+    return chunk // 256 if chunk % 256 == 0 else 1
 
 
 def kernel(
@@ -79,6 +83,8 @@
         gs[e * cap : (e + 1) * cap, :] = jnp.broadcast_to(gate, (cap, gs.shape[1]))
 
     tile = min(256, chunk)
+    pieces = pieces_of(chunk)
+    width = chunk // pieces
 
     def build(src, s):
         @pl.loop(0, chunk // tile)
@@ -90,18 +96,21 @@
     def rows(e):
         return pl.ds(pl.multiple_of(e * cap, cap), cap)
 
-    def exchange(s, dst, send, receive):
+    def exchange(s, dst, send, receive, sem=None, columns=pl.ds(0, chunk)):
+        sem = s if sem is None else sem
         for peer in epeer:
             pltpu.make_async_remote_copy(
-                src_ref=outgoing.at[s, rows(peer)],
-                dst_ref=dst.at[s, rows(me)],
-                send_sem=send.at[s],
-                recv_sem=receive.at[s],
+                src_ref=outgoing.at[s, rows(peer), columns],
+                dst_ref=dst.at[s, rows(me), columns],
+                send_sem=send.at[sem],
+                recv_sem=receive.at[sem],
                 device_id=(peer, mz),
                 device_id_type=MESH,
             ).start()
         pltpu.make_async_copy(
-            outgoing.at[s, rows(me)], dst.at[s, rows(me)], receive.at[s]
+            outgoing.at[s, rows(me), columns],
+            dst.at[s, rows(me), columns],
+            receive.at[sem],
         ).start()
 
     def wait_all(ref, sem):
@@ -189,21 +198,23 @@
     }
 
     def finish(s):
-        wait_all(orecv.at[s], out_recv.at[s])
         if s == 0:
             for q in range(1, nt):
                 p_copies[q].wait_recv()
-
-        @pl.loop(0, chunk // tile)
-        def _(c):
-            columns = pl.ds(pl.multiple_of(c * tile, tile), tile)
-            total = combine(s, columns)
-            if s == 0:
-                for q in range(1, nt):
-                    total = total + zrecv[q, :, columns].astype(jnp.float32)
-                out[:, columns] = total.astype(jnp.bfloat16)
-            else:
-                part[s, :, columns] = total.astype(jnp.bfloat16)
+        for piece in range(pieces):
+            here = pl.ds(piece * width, width)
+            wait_all(orecv.at[s, :, here], out_recv.at[s * pieces + piece])
+
+            @pl.loop(piece * (width // tile), (piece + 1) * (width // tile))
+            def _(c):
+                columns = pl.ds(pl.multiple_of(c * tile, tile), tile)
+                total = combine(s, columns)
+                if s == 0:
+                    for q in range(1, nt):
+                        total = total + zrecv[q, :, columns].astype(jnp.float32)
+                    out[:, columns] = total.astype(jnp.bfloat16)
+                else:
+                    part[s, :, columns] = total.astype(jnp.bfloat16)
 
         if s > 0:
             p_copies[s].start()
@@ -214,19 +225,23 @@
         weight_copy(1, s).wait()
         weight_copy(2, s).wait()
 
-        @pl.loop(0, chunk // tile)
-        def _(c):
-            columns = pl.ds(pl.multiple_of(c * tile, tile), tile)
-            term = dot(svt[0], wg[s, :, columns], NN)
-            term = term + dot(svt[1], wu[s, :, columns], NN)
-            outgoing[s, :, columns] = term.astype(jnp.bfloat16)
-
-        exchange(s, orecv, out_send, out_recv)
+        for piece in range(pieces):
+
+            @pl.loop(piece * (width // tile), (piece + 1) * (width // tile))
+            def _(c):
+                columns = pl.ds(pl.multiple_of(c * tile, tile), tile)
+                term = dot(svt[0], wg[s, :, columns], NN)
+                term = term + dot(svt[1], wu[s, :, columns], NN)
+                outgoing[s, :, columns] = term.astype(jnp.bfloat16)
+
+            here = pl.ds(piece * width, width)
+            exchange(s, orecv, out_send, out_recv, s * pieces + piece, here)
     for s in reversed(steps):
         finish(s)
 
-    for s in steps:
-        wait_all(others, out_send.at[s])
+    narrow = outgoing.at[0, pl.ds(0, (ne - 1) * cap), pl.ds(0, width)]
+    for unit in range(nt * pieces):
+        wait_all(narrow, out_send.at[unit])
     for s in range(1, nt):
         z_copies[s - 1].wait_send()
         p_copies[s].wait_send()
@@ -268,8 +283,8 @@
             dma((1,)),
             dma((nt,)),
             dma((nt,)),
-            dma((nt,)),
-            dma((nt,)),
+            dma((nt * pieces_of(chunk),)),
+            dma((nt * pieces_of(chunk),)),
             dma((nt,)),
             dma((nt,)),
             dma((nt,)),

time: 113 us -> 115 us (1.018)
  Pallas kernels: 111 us -> 113 us
    pallas_call x1, Pallas kernels: 111 us -> 113 us  [shards(): pl.pallas_call(functools.partial(kernel, ne, nt, cap), out_shape=jax.Shap...]
where the time goes in v3:
time: 115 us
  Pallas kernels  113 us (98%)
  local copies, waits for them, and re-layouts  1.67 us (1%)
    pallas_call x1, Pallas kernels, shards(): pl.pallas_call(functools.partial(kernel, ne, nt, cap), out_shape=jax.Shap...  113 us

profile of v3, /device:TPU:0, one launch (start us, length us, event | category | flops | bytes accessed | tf_op | source)
XLA Modules:
  0.0 114.9 jit_solution(8531591340185400354)
XLA Ops:
  0.0 113.2 %shard_map.82 = bf16[128,1024]{1,0:T(8,128)(2,1)} custom-call(bf16[128,1024]{1,0:T(8,128)(2,1)} %raw0.1, s32[4,128]{1,0:T(4,128)} %bitcast.3, f32[4,128]{1,0:T(4,128)} %bitcast.4, s32[1,128]{1,0:T(1,128)} %bitcast.5, bf16[1,1344,4096]{2,1,0:T(8,128)(2,1)} %w_gate.1, bf16[1,1344,4096]{2,1,0:T(8,128)(2,1)} %w_up.1, bf16[1,1344,4096]{2,1,0:T(8,128)(2,1)} %w_down.1, ...), custom_call_target="tpu_custom_call" | custom-call | tf_op jit(solution)/shard_map/pallas_call | solution.py:261
  113.2 1.7 %copy.10 = bf16[128,1024]{1,0:T(8,128)(2,1)} copy(bf16[128,1024]{1,0:T(8,128)(2,1)} %shard_map.82) | data formatting | bytes 524288
